TPU v7x, 32 devices: a whole 2x2x4 slice. The times are simulated.
32 devices in a mesh: lat: 4 (over y, core), lon: 8 (over z, x).
Axes of the slice: x: 2, y: 2, z: 4, core: 2. Of those that a mesh axis runs over, the one named last changes fastest.
Arguments:
- field: bfloat16 [64, 128, 384], P('lat', 'lon'), may hold values from -6 to 6
- obs_jac: bfloat16 [32, 32, 128, 384], P(None, ('lat', 'lon')), may hold values from -0.3125 to 0.3125
- obs_frac: bfloat16 [32, 32, 2, 128], P(None, ('lat', 'lon')), may hold values from 0 to 1
- obs_innov: bfloat16 [32, 32, 128], P(None, ('lat', 'lon')), may hold values from -6 to 6
- obs_rinv: bfloat16 [32, 32, 128], P(None, ('lat', 'lon')), may hold values from 1 to 16
- obs_cells: int32 [32, 32, 128], P(None, ('lat', 'lon')), may hold values from -1 to 270, as said below
Outputs:
- departures: float32 [32, 32, 128], P(None, ('lat', 'lon'))
- field_grad: float32 [64, 128, 384], P('lat', 'lon')
Inputs may be any that keep to these rules, and one draw needn't show every extreme that they name: `obs_cells`: in block (o, p) the live slots come first, at least one and at most 128; a live slot holds r * 17 + q with r below 16 and q below 16; slot 0 of every block holds the cell at r = 15, q = 15; the number of live slots varies by owner.
All inputs are finite; a program needn't handle non-finite values.
Results may differ from a plain program's by a relative error of at most 0.0046.
Values may be sent and summed in bfloat16 or wider, within the bound.
A program may use at most 128 MiB of HBM per device.

v0:
```python
import jax
import jax.numpy as jnp
from jax import lax
from jax.sharding import PartitionSpec as P


def shifted(block, axis, distance):
    devices = range(lax.axis_size(axis))
    route = [(i - distance, i) for i in devices if i - distance in devices]
    return lax.ppermute(block, axis, route)


def passed_along(value, axis, steps):
    count = lax.axis_size(axis)
    pairs = [(source, (source + steps) % count) for source in range(count)]
    return lax.ppermute(value, axis, pairs)


def bilinear_weights(frac_lat, frac_lon):
    lat_part = frac_lat.astype(jnp.float32)
    lon_part = frac_lon.astype(jnp.float32)
    raw_weights = (
        (1.0 - lat_part) * (1.0 - lon_part),
        lat_part * (1.0 - lon_part),
        (1.0 - lat_part) * lon_part,
        lat_part * lon_part,
    )
    return lax.optimization_barrier(tuple((weight.astype(jnp.bfloat16) for weight in raw_weights)))


def spread_matrix(cell_ids, frac_lat, frac_lon, stride, cells_total):
    is_live = cell_ids >= 0
    corner = jnp.where(is_live, cell_ids, 0)
    weights = bilinear_weights(frac_lat, frac_lon)
    cell_axis = lax.broadcasted_iota(jnp.int32, (1, cells_total), 1)
    matrix = jnp.zeros((cell_ids.shape[0], cells_total), jnp.float32)
    for weight, offset in zip(weights, (0, stride, 1, stride + 1)):
        live_weight = jnp.where(is_live, weight.astype(jnp.float32), 0.0)
        matrix = matrix + jnp.where(
            corner[:, None] + offset == cell_axis, live_weight[:, None], 0.0
        )
    return matrix.astype(jnp.bfloat16)


def forward_piece(spread, col_table, cell_ids, innovation, jacobian):
    interp = jnp.dot(spread, col_table, preferred_element_type=jnp.float32)
    evolved = jnp.sum(interp * jacobian.astype(jnp.float32), axis=1)
    return jnp.where(
        cell_ids >= 0, evolved - innovation.astype(jnp.float32), jnp.zeros((), jnp.float32)
    )


def adjoint_piece(spread, inv_error, departure, jacobian, grad_ext):
    contrib = (
        (inv_error.astype(jnp.float32) * departure)[:, None] * jacobian.astype(jnp.float32)
    ).astype(jnp.bfloat16)
    return grad_ext + lax.dot_general(
        spread, contrib, (((0,), (0,)), ((), ())), preferred_element_type=jnp.float32
    )


def shards(field, obs_jac, obs_frac, obs_innov, obs_rinv, obs_cells):
    lat_rows, lon_cols, width_all = field.shape
    north_row = shifted(field[:1], "lat", -1)
    taller = jnp.concatenate([field, north_row], axis=0)
    east_col = passed_along(taller[:, :1], "lon", -1)
    widened = jnp.concatenate([taller, east_col], axis=1)
    stride = lon_cols + 1
    col_table = widened.reshape(-1, width_all)
    cells_total = col_table.shape[0]
    jac_rows, frac_pair, innov_vals, rinv_vals = (
        lax.all_to_all(obs_jac, ("lat", "lon"), split_axis=0, concat_axis=1, tiled=True),
        lax.all_to_all(obs_frac, ("lat", "lon"), split_axis=0, concat_axis=1, tiled=True),
        lax.all_to_all(obs_innov, ("lat", "lon"), split_axis=0, concat_axis=1, tiled=True),
        lax.all_to_all(obs_rinv, ("lat", "lon"), split_axis=0, concat_axis=1, tiled=True),
    )
    cell_vals = lax.all_to_all(obs_cells, ("lat", "lon"), split_axis=0, concat_axis=1, tiled=True)
    sources = cell_vals.shape[1]
    slots_all = cell_vals.shape[2]
    cells_two = cell_vals.reshape(sources, slots_all)
    frac_three = frac_pair.reshape(sources, 2, slots_all)
    innov_two = innov_vals.reshape(sources, slots_all)
    rinv_two = rinv_vals.reshape(sources, slots_all)
    jac_three = jac_rows.reshape(sources, slots_all, width_all)
    piece = slots_all // 8
    piece_rows = sources * piece

    def take_piece(piece_idx):
        start = piece_idx * piece
        cells_p = lax.dynamic_slice_in_dim(cells_two, start, piece, 1).reshape(-1)
        frac_p = lax.dynamic_slice_in_dim(frac_three, start, piece, 2)
        lat_p = frac_p[:, 0, :].reshape(-1)
        lon_p = frac_p[:, 1, :].reshape(-1)
        innov_p = lax.dynamic_slice_in_dim(innov_two, start, piece, 1).reshape(-1)
        rinv_p = lax.dynamic_slice_in_dim(rinv_two, start, piece, 1).reshape(-1)
        jac_p = lax.dynamic_slice_in_dim(jac_three, start, piece, 1).reshape(piece_rows, width_all)
        return (cells_p, lat_p, lon_p, innov_p, rinv_p, jac_p)

    def store_piece(departs, departure, piece_idx):
        return lax.dynamic_update_slice_in_dim(
            departs, departure.reshape(sources, piece), piece_idx * piece, 1
        )

    def full_turn(piece_idx, state_pair):
        grad_ext, departs = state_pair
        cells_p, lat_p, lon_p, innov_p, rinv_p, jac_p = take_piece(piece_idx)
        spread = spread_matrix(cells_p, lat_p, lon_p, stride, cells_total)
        departure = forward_piece(spread, col_table, cells_p, innov_p, jac_p)
        grad_ext = adjoint_piece(spread, rinv_p, departure, jac_p, grad_ext)
        return (grad_ext, store_piece(departs, departure, piece_idx))

    grad_start = jnp.zeros((cells_total, width_all), jnp.float32)
    depart_start = jnp.zeros((sources, slots_all), jnp.float32)
    live_most = jnp.max(jnp.sum((cells_two >= 0).astype(jnp.int32), axis=1))
    pieces_used = (live_most + piece - 1) // piece
    grad_ext, departs = lax.fori_loop(0, pieces_used, full_turn, (grad_start, depart_start))
    grad_grid = grad_ext.reshape(lat_rows + 1, stride, width_all)
    east_back = passed_along(grad_grid[:, lon_cols:], "lon", 1)
    grad_grid = grad_grid[:, :lon_cols].at[:, :1].add(east_back)
    north_back = shifted(grad_grid[lat_rows:], "lat", 1)
    field_grad = grad_grid[:lat_rows].at[:1].add(north_back)
    departures = lax.all_to_all(
        departs.reshape(1, sources, slots_all),
        ("lat", "lon"),
        split_axis=1,
        concat_axis=0,
        tiled=True,
    )
    return (departures, field_grad)


def solution(mesh):
    placed = (
        P("lat", "lon", None),
        P(None, ("lat", "lon"), None, None),
        P(None, ("lat", "lon"), None, None),
        P(None, ("lat", "lon"), None),
        P(None, ("lat", "lon"), None),
        P(None, ("lat", "lon"), None),
    )
    return jax.shard_map(
        shards,
        mesh=mesh,
        in_specs=placed,
        out_specs=(P(None, ("lat", "lon"), None), P("lat", "lon", None)),
        check_vma=False,
    )
```

profile of v0, /device:TPU:0, one launch (start us, length us, event | category | flops | bytes accessed | tf_op | source)
XLA Modules:
  0.0 183.7 jit_solution(12065559047575675687)
XLA Ops:
  0.6 1.3 copy.22
  1.9 7.3 %all-to-all-start.4 = ((bf16[32,1,128]{2,1,0:T(2,128)(2,1)}), bf16[32,1,128]{2,1,0:T(2,128)(2,1)S(1)}, u32[]{:S(2)}, u32[]{:S(2)}) async-start(bf16[32,1,128]{2,1,0:T(2,128)(2,1)} %copy.22), calls=%async_computation.4 | async-start | bytes 32768 | tf_op jit(solution)/shard_map/all_to_all | solution.py:74
  9.3 0.7 copy.21
  10.0 6.4 %all-to-all-done.4 = bf16[32,1,128]{2,1,0:T(2,128)(2,1)S(1)} async-done(((bf16[32,1,128]{2,1,0:T(2,128)(2,1)}), bf16[32,1,128]{2,1,0:T(2,128)(2,1)S(1)}, u32[]{:S(2)}, u32[]{:S(2)}) %all-to-all-start.4) | async-done | bytes 8224 | tf_op jit(solution)/shard_map/all_to_all | solution.py:74
  16.3 8.8 %all_to_all.27 = bf16[32,1,128]{2,1,0:T(2,128)(2,1)S(1)} all-to-all(bf16[32,1,128]{2,1,0:T(2,128)(2,1)S(1)} %copy.21), channel_id=1, replica_groups=mesh['lat'=4,'lon'=8] {'lat','lon'}, dimensions={0} | all-to-all | bytes 16384 | tf_op jit(solution)/shard_map/all_to_all | solution.py:75
  25.2 9.6 %all_to_all.28 = s32[32,1,128]{2,1,0:T(1,128)S(1)} all-to-all(s32[32,1,128]{2,1,0:T(1,128)} %param.17), channel_id=1, replica_groups=mesh['lat'=4,'lon'=8] {'lat','lon'}, dimensions={0} | all-to-all | bytes 32768 | tf_op jit(solution)/shard_map/all_to_all | solution.py:77
  34.8 9.6 %all_to_all.29 = bf16[32,1,2,128]{3,2,1,0:T(2,128)(2,1)S(1)} all-to-all(bf16[32,1,2,128]{3,2,1,0:T(2,128)(2,1)} %param.14), channel_id=1, replica_groups=mesh['lat'=4,'lon'=8] {'lat','lon'}, dimensions={0} | all-to-all | bytes 32768 | tf_op jit(solution)/shard_map/all_to_all | solution.py:73
  44.4 3.7 %all-to-all-start.3 = ((bf16[32,1,128,384]{3,2,1,0:T(8,128)(2,1)}), bf16[32,1,128,384]{3,2,1,0:T(8,128)(2,1)}, u32[]{:S(2)}, u32[]{:S(2)}) async-start(bf16[32,1,128,384]{3,2,1,0:T(8,128)(2,1)} %param.13), calls=%async_computation.3 | async-start | bytes 6291456 | tf_op jit(solution)/shard_map/all_to_all | solution.py:72
  48.1 1.3 collective-permute-start
  49.4 1.7 collective-permute-done
  51.2 4.5 %collective-permute-start.1 = (bf16[17,1,384]{2,1,0:T(2,128)(2,1)S(1)}, bf16[17,1,384]{2,1,0:T(2,128)(2,1)S(1)}, u32[]{:S(2)}, u32[]{:S(2)}) collective-permute-start(bf16[17,1,384]{2,1,0:T(2,128)(2,1)S(1)} %slice.82), channel_id=1, source_target_pairs={{0,7},{1,0},{2,1},{3,2},{4,3},{5,4},{6,5},{7,6},{8,15},{9,8},{10,9... | collective-permute-start | bytes 39176 | tf_op jit(solution)/shard_map/ppermute | solution.py:16
  55.7 44.9 %collective-permute-done.1 = bf16[17,1,384]{2,1,0:T(2,128)(2,1)S(1)} collective-permute-done((bf16[17,1,384]{2,1,0:T(2,128)(2,1)S(1)}, bf16[17,1,384]{2,1,0:T(2,128)(2,1)S(1)}, u32[]{:S(2)}, u32[]{:S(2)}) %collective-permute-start.1) | collective-permute-done | bytes 13088 | tf_op jit(solution)/shard_map/ppermute | solution.py:16
  100.8 0.1 convert_reduce_fusion
  100.9 0.6 reduce_max.9
  102.2 18.4 %all-to-all-done.3 = bf16[32,1,128,384]{3,2,1,0:T(8,128)(2,1)} async-done(((bf16[32,1,128,384]{3,2,1,0:T(8,128)(2,1)}), bf16[32,1,128,384]{3,2,1,0:T(8,128)(2,1)}, u32[]{:S(2)}, u32[]{:S(2)}) %all-to-all-start.3) | async-done | bytes 3145760 | tf_op jit(solution)/shard_map/all_to_all | solution.py:72
  120.6 0.6 broadcast_in_dim.59
  121.2 25.1 %while.14 = (s32[]{:T(128)}, f32[289,384]{1,0:T(8,128)S(1)}, f32[32,128]{1,0:T(8,128)}, s32[]{:T(128)}, s32[32,128]{1,0:T(8,128)S(1)}, /*index=5*/bf16[32,2,128]...) while((s32[]{:T(128)}, f32[289,384]{1,0:T(8,128)S(1)}, ...), condition=%wide.region_4.5_spmd, body=%wide.region_2.4_spmd.sunk | while | flops 231940992 | bytes 6360035 | solution.py:116
  121.2 0.1 constant_dynamic-slice_fusion.8
  121.7 1.1 constant_dynamic-slice_fusion.7
  122.9 0.3 copy.39
  123.2 1.4 fusion.9
  124.8 1.1 convolution_add_fusion.2
  126.1 1.3 dynamic_update_slice.4
  127.4 0.1 constant_dynamic-slice_fusion.8
  127.9 1.1 constant_dynamic-slice_fusion.7
  129.1 0.3 copy.39
  129.4 1.4 fusion.9
  131.1 1.1 convolution_add_fusion.2
  132.3 1.4 dynamic_update_slice.4
  133.7 0.1 constant_dynamic-slice_fusion.8
  134.2 1.1 constant_dynamic-slice_fusion.7
  135.3 0.1 bitcast_convert_fusion.2
  135.4 0.3 copy.39
  135.7 1.4 fusion.9
  137.3 1.1 convolution_add_fusion.2
  138.6 1.4 dynamic_update_slice.4
  140.0 0.1 constant_dynamic-slice_fusion.8
  140.5 1.1 constant_dynamic-slice_fusion.7
  141.7 0.3 copy.39
  142.0 1.4 fusion.9
  143.6 1.1 convolution_add_fusion.2
  144.9 1.4 dynamic_update_slice.4
  146.5 29.4 %all-to-all-start.5 = ((f32[1,32,128]{2,0,1:T(1,128)}), f32[1,32,128]{2,0,1:T(1,128)S(1)}, u32[]{:S(2)}, u32[]{:S(2)}) async-start(f32[1,32,128]{2,0,1:T(1,128)} %bitcast.4), calls=%async_computation.5 | async-start | bytes 32768 | tf_op jit(solution)/shard_map/all_to_all | solution.py:122
  176.0 0.1 scatter-add.6
  176.1 2.8 %collective-permute-start.3 = (f32[1,16,384]{2,1,0:T(8,128)S(1)}, f32[1,16,384]{2,1,0:T(8,128)S(1)}, u32[]{:S(2)}, u32[]{:S(2)}) collective-permute-start(f32[1,16,384]{2,1,0:T(8,128)S(1)} %slice.88), channel_id=1, source_target_pairs={{0,8},{8,16},{16,24},{1,9},{9,17},{17,25},{2,10},{10,18},{18,26},{... | collective-permute-start | bytes 73736 | tf_op jit(solution)/shard_map/ppermute | solution.py:10
  178.9 4.1 %all-to-all-done.5 = f32[1,32,128]{2,0,1:T(1,128)S(1)} async-done(((f32[1,32,128]{2,0,1:T(1,128)}), f32[1,32,128]{2,0,1:T(1,128)S(1)}, u32[]{:S(2)}, u32[]{:S(2)}) %all-to-all-start.5) | async-done | bytes 16416 | tf_op jit(solution)/shard_map/all_to_all | solution.py:122
  183.0 0.6 copy.54
  183.7 0.1 copy-done
  (89 shorter events, 3.8 us)
Async XLA Ops:
  1.9 14.4 %all-to-all-start.4 = ((bf16[32,1,128]{2,1,0:T(2,128)(2,1)}), bf16[32,1,128]{2,1,0:T(2,128)(2,1)S(1)}, u32[]{:S(2)}, u32[]{:S(2)}) async-start(bf16[32,1,128]{2,1,0:T(2,128)(2,1)} %copy.22), calls=%async_computation.4 | async-start | bytes 32768 | tf_op jit(solution)/shard_map/all_to_all | solution.py:74
  44.4 3.7 %copy-start.1 = (bf16[16,16,384]{2,1,0:T(8,128)(2,1)S(1)}, bf16[16,16,384]{2,1,0:T(8,128)(2,1)}, u32[]{:S(2)}) copy-start(bf16[16,16,384]{2,1,0:T(8,128)(2,1)} %param.12) | copy-start | bytes 589828
  44.4 76.2 %all-to-all-start.3 = ((bf16[32,1,128,384]{3,2,1,0:T(8,128)(2,1)}), bf16[32,1,128,384]{3,2,1,0:T(8,128)(2,1)}, u32[]{:S(2)}, u32[]{:S(2)}) async-start(bf16[32,1,128,384]{3,2,1,0:T(8,128)(2,1)} %param.13), calls=%async_computation.3 | async-start | bytes 6291456 | tf_op jit(solution)/shard_map/all_to_all | solution.py:72
  48.1 3.1 %collective-permute-start = (bf16[1,16,384]{2,1,0:T(8,128)(2,1)S(1)}, bf16[1,16,384]{2,1,0:T(8,128)(2,1)S(1)}, u32[]{:S(2)}, u32[]{:S(2)}) collective-permute-start(bf16[1,16,384]{2,1,0:T(8,128)(2,1)S(1)} %slice.74), channel_id=1, source_target_pairs={{8,0},{16,8},{24,16},{9,1},{17,9},{25,17},{10,2},{18,10},{26,18},{... | collective-permute-start | bytes 36872 | tf_op jit(solution)/shard_map/ppermute | solution.py:10
  51.2 49.5 %collective-permute-start.1 = (bf16[17,1,384]{2,1,0:T(2,128)(2,1)S(1)}, bf16[17,1,384]{2,1,0:T(2,128)(2,1)S(1)}, u32[]{:S(2)}, u32[]{:S(2)}) collective-permute-start(bf16[17,1,384]{2,1,0:T(2,128)(2,1)S(1)} %slice.82), channel_id=1, source_target_pairs={{0,7},{1,0},{2,1},{3,2},{4,3},{5,4},{6,5},{7,6},{8,15},{9,8},{10,9... | collective-permute-start | bytes 39176 | tf_op jit(solution)/shard_map/ppermute | solution.py:16
  146.4 29.5 %collective-permute-start.2 = (f32[17,1,384]{2,1,0:T(1,128)S(1)}, f32[17,1,384]{2,1,0:T(1,128)S(1)}, u32[]{:S(2)}, u32[]{:S(2)}) collective-permute-start(f32[17,1,384]{2,1,0:T(1,128)S(1)} %slice.85), channel_id=1, source_target_pairs={{0,1},{1,2},{2,3},{3,4},{4,5},{5,6},{6,7},{7,0},{8,9},{9,10},{10,1... | collective-permute-start | bytes 78344 | tf_op jit(solution)/shard_map/ppermute | solution.py:16
  146.5 36.5 %all-to-all-start.5 = ((f32[1,32,128]{2,0,1:T(1,128)}), f32[1,32,128]{2,0,1:T(1,128)S(1)}, u32[]{:S(2)}, u32[]{:S(2)}) async-start(f32[1,32,128]{2,0,1:T(1,128)} %bitcast.4), calls=%async_computation.5 | async-start | bytes 32768 | tf_op jit(solution)/shard_map/all_to_all | solution.py:122
  176.1 6.9 %collective-permute-start.3 = (f32[1,16,384]{2,1,0:T(8,128)S(1)}, f32[1,16,384]{2,1,0:T(8,128)S(1)}, u32[]{:S(2)}, u32[]{:S(2)}) collective-permute-start(f32[1,16,384]{2,1,0:T(8,128)S(1)} %slice.88), channel_id=1, source_target_pairs={{0,8},{8,16},{16,24},{1,9},{9,17},{17,25},{2,10},{10,18},{18,26},{... | collective-permute-start | bytes 73736 | tf_op jit(solution)/shard_map/ppermute | solution.py:10
  183.0 0.8 copy-start
where the time goes:
time: 185 us; the launch traced here: 184 us
  waiting for transfers between devices  75.5 us (41%)
  starting transfers between devices  49 us (26%)
  blocking collectives  28 us (15%)
  local copies, waits for them, and re-layouts  17.3 us (9%)
  matrix products  10.1 us (5%)
  other arithmetic  2.04 us (1%)
    ppermute x2, waiting for transfers between devices, passed_along(): return lax.ppermute(value, axis, pairs)  44.9 us
    all_to_all x1, starting transfers between devices, shards(): lax.all_to_all(departs.reshape(1, sources, slots_all), ('lat', 'lon'), sp...  29.4 us
    all_to_all x1, waiting for transfers between devices, shards(): lax.all_to_all(obs_jac, ('lat', 'lon'), split_axis=0, concat_axis=1, tile...  18.4 us
    all_to_all x1, blocking collectives, shards(): lax.all_to_all(obs_cells, ('lat', 'lon'), split_axis=0, concat_axis=1, ti...  9.61 us
    all_to_all x1, blocking collectives, shards(): lax.all_to_all(obs_frac, ('lat', 'lon'), split_axis=0, concat_axis=1, til...  9.61 us
    all_to_all x1, blocking collectives, shards(): lax.all_to_all(obs_rinv, ('lat', 'lon'), split_axis=0, concat_axis=1, til...  8.82 us
    all_to_all x1, starting transfers between devices, shards(): lax.all_to_all(obs_innov, ('lat', 'lon'), split_axis=0, concat_axis=1, ti...  7.33 us
    all_to_all x1, waiting for transfers between devices, shards(): lax.all_to_all(obs_innov, ('lat', 'lon'), split_axis=0, concat_axis=1, ti...  6.35 us
  transfers between devices with their start and end apart: 7, of which 5 were waited for; matrix products, arithmetic and copies ran while one was open for 1% of the time, Pallas kernels for 0%

commit v1 on v0

v1 whole, which is shorter than its diff:
```python
import functools
import math

import jax
import jax.numpy as jnp
from jax import lax
from jax.experimental import pallas as pl
from jax.experimental.pallas import tpu as pltpu
from jax.sharding import PartitionSpec as P

MESH = pl.DeviceIdType.MESH


def weight_rows(position, frac, rows):
    ids = lax.broadcasted_iota(jnp.int32, (rows, position.shape[1]), 0).astype(jnp.float32)
    zero = jnp.zeros_like(ids)
    return jnp.where(
        ids == position, 1.0 - frac, jnp.where(ids == position + 1.0, frac, zero)
    )


def kernel(
    lat_n, lon_n, line, rows, cols, tile,
    field, edge, meta, jac,
    grad_out, dep_out,
    tbl, met, jrecv, dep, grad, gsend, grecv, hrecv,
    t_send, t_recv, m_send, m_recv, j_send, j_recv, d_send, d_recv,
    g_send, g_recv, h_send, h_recv,
):
    inner = lon_n // line
    plane = lat_n * inner
    total = lat_n * lon_n
    slots = jac.shape[3]
    cells = rows * cols
    lat, lon = lax.axis_index("lat"), lax.axis_index("lon")
    z, xi = lon // inner, lon % inner
    here = lat * inner + xi
    lat_up, lat_down = (lat + 1) % lat_n, (lat + lat_n - 1) % lat_n
    lon_up, lon_down = (lon + 1) % lon_n, (lon + lon_n - 1) % lon_n

    def remote(src, dst, send, recv, to):
        return pltpu.make_async_remote_copy(
            src_ref=src, dst_ref=dst, send_sem=send, recv_sem=recv,
            device_id=to, device_id_type=MESH,
        )

    def landed(dst, sem):
        pltpu.make_async_copy(dst, dst, sem).wait()

    me = lat * lon_n + lon
    barrier = pltpu.get_barrier_semaphore()

    def greet(i, carry):
        other = (me + i) % total
        pl.semaphore_signal(
            barrier, inc=1, device_id=(other // lon_n, other % lon_n), device_id_type=MESH
        )
        return carry

    lax.fori_loop(1, total, greet, 0)

    own_tbl = pltpu.make_async_copy(field, tbl.at[z, pl.ds(0, cells)], t_recv.at[0, z])
    own_tbl.start()
    own_met = pltpu.make_async_copy(
        meta.at[lat, :, xi], met.at[:, :, pl.ds(here * slots, slots)], m_recv.at[here]
    )
    own_met.start()

    def own_jac(g, carry):
        pltpu.make_async_copy(
            jac.at[lat, g, xi], jrecv.at[g, pl.ds(here * slots, slots)], j_recv.at[g, here]
        ).start()
        return carry

    lax.fori_loop(0, line, own_jac, 0)
    pl.semaphore_wait(barrier, total - 1)

    z_low, x_low = lon_down // inner, lon_down % inner
    halo = cells + cols

    def table_copies(i):
        to = (z + i) % line
        return (
            remote(field, tbl.at[z, pl.ds(0, cells)], t_send.at[0, to], t_recv.at[0, z],
                   (lat, to * inner + xi)),
            remote(field.at[pl.ds(0, cols)], tbl.at[z, pl.ds(cells, cols)],
                   t_send.at[1, to], t_recv.at[1, z], (lat_down, to * inner + xi)),
            remote(edge, tbl.at[z_low, pl.ds(halo, rows)], t_send.at[2, to],
                   t_recv.at[2, z_low], (lat, to * inner + x_low)),
            remote(edge, tbl.at[z_low, pl.ds(halo + rows, rows)], t_send.at[3, to],
                   t_recv.at[3, z_low], (lat_down, to * inner + x_low)),
        )

    def meta_copy(i):
        to = (here + i) % plane
        return remote(
            meta.at[to // inner, :, to % inner], met.at[:, :, pl.ds(here * slots, slots)],
            m_send.at[to], m_recv.at[here], (to // inner, z * inner + to % inner),
        )

    def jac_copy(g, i):
        to = (here + i) % plane
        return remote(
            jac.at[to // inner, g, to % inner], jrecv.at[g, pl.ds(here * slots, slots)],
            j_send.at[g, to], j_recv.at[g, here], (to // inner, z * inner + to % inner),
        )

    def dep_copy(g, i):
        to = (here + i) % plane
        return remote(
            dep.at[g, :, pl.ds(to * slots, slots)], dep_out.at[lat, g, xi],
            d_send.at[g, to], d_recv.at[lat, g, xi], (to // inner, z * inner + to % inner),
        )

    def main_copy(g):
        return remote(gsend.at[g, pl.ds(0, cells)], grecv.at[z], g_send.at[g], g_recv.at[z],
                      (lat, g * inner + xi))

    def halo_copies(g):
        east = (g * inner + xi + 1) % lon_n
        return (
            remote(gsend.at[g, pl.ds(cells, cols)], hrecv.at[0, z], h_send.at[0, g],
                   h_recv.at[0, z], (lat_up, g * inner + xi)),
            remote(gsend.at[g, pl.ds(halo, rows)], hrecv.at[1, z], h_send.at[1, g],
                   h_recv.at[1, z], (lat, east)),
            remote(gsend.at[g, pl.ds(halo + rows, rows)], hrecv.at[2, z], h_send.at[2, g],
                   h_recv.at[2, z], (lat_up, east)),
        )

    def send_meta(i, carry):
        meta_copy(i).start()
        return carry

    def send_tables(i, carry):
        main, north, east, corner = table_copies(i)
        main.start()
        north.start()
        east.start()
        corner.start()
        return carry

    def send_jac(n, carry):
        jac_copy((z + 1 + n // (plane - 1)) % line, 1 + n % (plane - 1)).start()
        return carry

    lax.fori_loop(1, plane, send_meta, 0)
    lax.fori_loop(1, line, send_tables, 0)
    _, north, east, corner = table_copies(0)
    north.start()
    east.start()
    corner.start()
    lax.fori_loop(0, line * (plane - 1), send_jac, 0)

    def wait_meta(k, carry):
        landed(met.at[:, :, pl.ds(k * slots, slots)], m_recv.at[k])
        return carry

    lax.fori_loop(0, plane, wait_meta, 0)
    inside = jnp.where(lat < lat_n - 1, 1.0, 0.0)
    width = tile * slots
    pad = -(-(max(rows, cols) + 1) // 8) * 8

    def group(n, carry):
        g = (z + 1 + n) % line
        landed(tbl.at[g, pl.ds(0, cells)], t_recv.at[0, g])
        landed(tbl.at[g, pl.ds(cells, cols)], t_recv.at[1, g])
        landed(tbl.at[g, pl.ds(halo, rows)], t_recv.at[2, g])
        landed(tbl.at[g, pl.ds(halo + rows, rows)], t_recv.at[3, g])

        def wait_jac(k, inner_carry):
            landed(jrecv.at[g, pl.ds(k * slots, slots)], j_recv.at[g, k])
            return inner_carry

        lax.fori_loop(0, plane, wait_jac, 0)
        grad[...] = jnp.zeros_like(grad)

        def one_tile(t, inner_carry):
            lanes = pl.ds(pl.multiple_of(t * width, width), width)
            info = met[g, :, lanes]
            lat_w = weight_rows(info[0:1], info[2:3], pad)
            lon_w = weight_rows(info[1:2], info[3:4], pad)
            lon_c = lon_w[:cols]
            lon_e = lon_w[cols:cols + 1]
            lat_n_row = lat_w[rows:rows + 1] * inside
            first = lax.broadcasted_iota(jnp.int32, (rows, width), 0) == 0
            blocks = [lat_w[r:r + 1] * lon_c for r in range(rows)]
            blocks.append(lat_n_row * lon_c)
            blocks.append(lat_w[:rows] * lon_e)
            blocks.append(
                jnp.where(first, jnp.broadcast_to(lat_n_row * lon_e, (rows, width)), 0.0)
            )
            spread = jnp.concatenate(blocks, axis=0).astype(jnp.bfloat16).astype(jnp.float32)
            jac_t = jrecv[g, lanes]
            products = lax.dot_general(
                tbl[g], jac_t, (((1,), (1,)), ((), ())), preferred_element_type=jnp.float32
            )
            evolved = jnp.sum(spread * products, axis=0, keepdims=True)
            departure = jnp.where(info[0:1] >= 0.0, evolved - info[4:5], 0.0)
            dep[g, :, lanes] = departure
            scaled = (spread * (info[5:6] * departure)).astype(jnp.bfloat16)
            grad[...] += jnp.dot(scaled, jac_t, preferred_element_type=jnp.float32)
            return inner_carry

        lax.fori_loop(0, plane // tile, one_tile, 0)
        gsend[g] = grad[...].astype(jnp.bfloat16)

        @pl.when(n < line - 1)
        def _():
            main_copy(g).start()

        for copy in halo_copies(g):
            copy.start()

        def send_dep(i, inner_carry):
            dep_copy(g, i).start()
            return inner_carry

        lax.fori_loop(1, plane, send_dep, 0)
        pltpu.make_async_copy(
            dep.at[g, :, pl.ds(here * slots, slots)], dep_out.at[lat, g, xi],
            d_recv.at[lat, g, xi],
        ).start()
        return carry

    lax.fori_loop(0, line, group, 0)

    grad_out[...] = grad[pl.ds(0, cells), :]

    def add_main(i, carry):
        source = (z + i) % line
        landed(grecv.at[source], g_recv.at[source])
        grad_out[...] += grecv[source].astype(jnp.float32)
        return carry

    lax.fori_loop(1, line, add_main, 0)

    def add_halo(s, carry):
        landed(hrecv.at[0, s], h_recv.at[0, s])
        landed(hrecv.at[1, s], h_recv.at[1, s])
        landed(hrecv.at[2, s], h_recv.at[2, s])
        return carry

    lax.fori_loop(0, line, add_halo, 0)
    grad_out[pl.ds(0, cols), :] += jnp.sum(hrecv[0].astype(jnp.float32), axis=0)
    east_sum = jnp.sum(hrecv[1].astype(jnp.float32), axis=0)
    corner_sum = jnp.sum(hrecv[2].astype(jnp.float32), axis=0)
    for r in range(rows):
        extra = east_sum[r:r + 1]
        if r == 0:
            extra = extra + corner_sum[0:1]
        grad_out[pl.ds(r * cols, 1), :] += extra

    def end_dep_recv(n, carry):
        k, g = n // line, n % line
        landed(dep_out.at[k // inner, g, k % inner], d_recv.at[k // inner, g, k % inner])
        return carry

    lax.fori_loop(0, plane * line, end_dep_recv, 0)

    def end_tables(i, carry):
        for copy in table_copies(i):
            copy.wait_send()
        return carry

    lax.fori_loop(1, line, end_tables, 0)
    north.wait_send()
    east.wait_send()
    corner.wait_send()

    def end_meta(i, carry):
        meta_copy(i).wait_send()
        return carry

    lax.fori_loop(1, plane, end_meta, 0)

    def end_blocks(n, carry):
        g, i = n // (plane - 1), 1 + n % (plane - 1)
        jac_copy(g, i).wait_send()
        dep_copy(g, i).wait_send()
        return carry

    lax.fori_loop(0, line * (plane - 1), end_blocks, 0)

    def end_main(i, carry):
        main_copy((z + i) % line).wait_send()
        return carry

    lax.fori_loop(1, line, end_main, 0)

    def end_halo(g, carry):
        for copy in halo_copies(g):
            copy.wait_send()
        return carry

    lax.fori_loop(0, line, end_halo, 0)


def shards(mesh_shape, field, obs_jac, obs_frac, obs_innov, obs_rinv, obs_cells):
    lat_n, lon_n = mesh_shape
    line = math.gcd(lon_n // 2, 4)
    inner = lon_n // line
    plane = lat_n * inner
    rows, cols, wide = field.shape
    slots = obs_jac.shape[2]
    tile = math.gcd(plane, 4)
    cells = rows * cols
    table = cells + cols + 2 * rows

    ids = obs_cells[:, 0]
    live = ids >= 0
    f32 = jnp.float32
    away = jnp.asarray(-1000.0, f32)
    row_pos = jnp.where(live, (ids // (cols + 1)).astype(f32), away)
    col_pos = jnp.where(live, (ids % (cols + 1)).astype(f32), away)
    none = jnp.zeros_like(row_pos)
    meta = jnp.stack(
        [row_pos, col_pos, obs_frac[:, 0, 0].astype(f32), obs_frac[:, 0, 1].astype(f32),
         obs_innov[:, 0].astype(f32), obs_rinv[:, 0].astype(f32), none, none],
        axis=1,
    ).reshape(lat_n, line, inner, 8, slots)
    jac = obs_jac.reshape(lat_n, line, inner, slots, wide)
    bf16 = jnp.bfloat16
    dma = pltpu.SemaphoreType.DMA
    vmem = pl.BlockSpec(memory_space=pltpu.VMEM)
    grad, departures = pl.pallas_call(
        functools.partial(kernel, lat_n, lon_n, line, rows, cols, tile),
        out_shape=(
            jax.ShapeDtypeStruct((cells, wide), f32),
            jax.ShapeDtypeStruct((lat_n, line, inner, 1, slots), f32),
        ),
        in_specs=[vmem, vmem, vmem, pl.BlockSpec(memory_space=pl.ANY)],
        out_specs=(vmem, vmem),
        scratch_shapes=[
            pltpu.VMEM((line, table, wide), bf16),
            pltpu.VMEM((line, 8, plane * slots), f32),
            pltpu.VMEM((line, plane * slots, wide), bf16),
            pltpu.VMEM((line, 1, plane * slots), f32),
            pltpu.VMEM((table, wide), f32),
            pltpu.VMEM((line, table, wide), bf16),
            pltpu.VMEM((line, cells, wide), bf16),
            pltpu.VMEM((3, line, rows, wide), bf16),
            dma((4, line)), dma((4, line)),
            dma((plane,)), dma((plane,)),
            dma((line, plane)), dma((line, plane)),
            dma((line, plane)), dma((lat_n, line, inner)),
            dma((line,)), dma((line,)),
            dma((3, line)), dma((3, line)),
        ],
        compiler_params=pltpu.CompilerParams(
            collective_id=0, has_side_effects=True, vmem_limit_bytes=60 * 1024 * 1024
        ),
    )(field.reshape(cells, wide), field[:, 0], meta, jac)
    return (
        departures.reshape(lat_n * lon_n, 1, slots),
        grad.reshape(rows, cols, wide),
    )


def solution(mesh):
    placed = (
        P("lat", "lon", None),
        P(None, ("lat", "lon"), None, None),
        P(None, ("lat", "lon"), None, None),
        P(None, ("lat", "lon"), None),
        P(None, ("lat", "lon"), None),
        P(None, ("lat", "lon"), None),
    )
    return jax.shard_map(
        functools.partial(shards, (mesh.shape["lat"], mesh.shape["lon"])),
        mesh=mesh,
        in_specs=placed,
        out_specs=(P(None, ("lat", "lon"), None), P("lat", "lon", None)),
        check_vma=False,
    )
```

time: 185 us -> 66.9 us (0.36)
  waiting for transfers between devices: 75.5 us -> 0 us
  Pallas kernels: 0 us -> 57 us
  starting transfers between devices: 49 us -> 0 us
  blocking collectives: 28 us -> 0 us
  local copies, waits for them, and re-layouts: 17.3 us -> 6.25 us
  matrix products: 10.1 us -> 0 us
    pallas_call x0 -> x1, Pallas kernels: none -> 57 us  [shards(): pl.pallas_call(functools.partial(kernel, lat_n, lon_n, line, rows, cols,...]
    ppermute x4 -> x0, waiting for transfers between devices: 46.7 us -> none  [the longest x2 44.9 us: passed_along(): return lax.ppermute(value, axis, pairs)]
    all_to_all x3 -> x0, starting transfers between devices: 40.4 us -> none  [the longest x1 29.4 us: shards(): lax.all_to_all(departs.reshape(1, sources, slots_all), ('lat', 'lon'), sp...]
    all_to_all x3 -> x0, waiting for transfers between devices: 28.8 us -> none  [the longest x1 18.4 us: shards(): lax.all_to_all(obs_jac, ('lat', 'lon'), split_axis=0, concat_axis=1, tile...]
    all_to_all x3 -> x0, blocking collectives: 28 us -> none  [the longest x1 9.61 us: shards(): lax.all_to_all(obs_cells, ('lat', 'lon'), split_axis=0, concat_axis=1, ti...]
    dot_general x8 -> x0, matrix products: 10.1 us -> none  [the longest x4 5.68 us: forward_piece(): interp = jnp.dot(spread, col_table, preferred_element_type=jnp.float32)]
    ppermute x4 -> x0, starting transfers between devices: 8.62 us -> none  [the longest x2 4.58 us: passed_along(): return lax.ppermute(value, axis, pairs)]
    dynamic_update_slice x4 -> x0, local copies, waits for them, and re-layouts: 5.59 us -> none  [store_piece(): lax.dynamic_update_slice_in_dim(departs, departure.reshape(sources, piece...]
  transfers between devices with their start and end apart: 7 -> 0, of which waited for: 5 -> 0; matrix products, arithmetic and copies ran while one was open for 1% -> 0% of each run, Pallas kernels for 0% -> 0%
where the time goes in v1:
time: 66.9 us; the launch traced here: 66.2 us
  Pallas kernels  57 us (85%)
  local copies, waits for them, and re-layouts  6.25 us (9%)
  other arithmetic  2.27 us (3%)
    pallas_call x1, Pallas kernels, shards(): pl.pallas_call(functools.partial(kernel, lat_n, lon_n, line, rows, cols,...  57 us
    unnamed x3, local copies, waits for them, and re-layouts  3.69 us
    another operation x2, other arithmetic, shards(): jnp.stack([row_pos, col_pos, obs_frac[:, 0, 0].astype(f32), obs_frac[:, 0...  1.4 us

profile of v1, /device:TPU:0, one launch (start us, length us, event | category | flops | bytes accessed | tf_op | source)
XLA Modules:
  0.0 66.2 jit_solution(2642584072357426177)
XLA Ops:
  0.6 0.7 %stack.32 = f32[32,1,128]{2,0,1:T(8,128)S(1)} convert(bf16[32,1,128]{2,0,1:T(8,128)(2,1)} %param.9) | non-fusion elementwise | flops 4096 | bytes 24576 | tf_op jit(solution)/shard_map/stack | solution.py:316
  1.3 0.7 %stack.33 = f32[32,1,128]{2,0,1:T(8,128)S(1)} convert(bf16[32,1,128]{2,0,1:T(8,128)(2,1)} %param.10) | non-fusion elementwise | flops 4096 | bytes 24576 | tf_op jit(solution)/shard_map/stack | solution.py:316
  2.0 0.9 %slice.9 = bf16[16,1,384]{2,1,0:T(2,128)(2,1)S(1)} slice(bf16[16,16,384]{2,1,0:T(8,128)(2,1)} %param.6), slice={[0:16], [0:1], [0:384]} | slice | bytes 24576 | tf_op jit(solution)/shard_map/slice | solution.py:352
  2.9 0.6 copy.12
  3.5 0.8 %fusion.1 = (bf16[32,1,1,128]{3,2,1,0:T(2,128)(2,1)S(1)}, bf16[32,1,1,128]{3,2,1,0:T(2,128)(2,1)S(1)}) fusion(bf16[32,1,2,128]{3,2,1,0:T(2,128)(2,1)} %param.8), kind=kLoop, calls=%fused_computation.6 | loop fusion | bytes 32768 | tf_op jit(solution)/shard_map/slice | solution.py:317
  4.4 0.9 %compare_select_fusion = (f32[32,1,128]{2,1,0:T(1,128)S(1)}, f32[32,1,128]{2,1,0:T(1,128)S(1)}) fusion(s32[32,1,128]{2,1,0:T(1,128)} %param.11), kind=kLoop, calls=%fused_computation.2 | loop fusion | flops 69632 | bytes 49152 | tf_op jit(solution)/shard_map/jit(_where)/select_n | solution.py:314
  5.3 0.8 %stack.31.meta = f32[4,4,2,8,128]{4,3,2,1,0:T(8,128)} concatenate(f32[4,4,2,1,128]{4,3,2,1,0:T(1,128)S(1)} %bitcast.21, f32[4,4,2,1,128]{4,3,2,1,0:T(1,128)S(1)} %bitcast.20, bf16[4,4,2,1,128]{4,3,2,1,0:T(2,128)(2,1)S(1)} %bitcast.25, bf16[4,4,2,1,128]{4,3,2,1,0:T(2,128)(2,1)S(1)} %bitcast.24, f32[4,4,2,1,128]{4,3,2,1,0:T(1,128)S(1)} %bitcast.22, ...), dimensions={3} | concatenate | bytes 245760 | tf_op jit(solution)/shard_map/stack | solution.py:316
  6.1 57.0 %shard_map.77 = (f32[256,384]{1,0:T(8,128)}, f32[4,4,2,1,128]{4,3,2,1,0:T(1,128)}) custom-call(bf16[256,384]{1,0:T(8,128)(2,1)} %bitcast.19, bf16[16,384]{1,0:T(8,128)(2,1)} %bitcast.26, f32[4,4,2,8,128]{4,3,2,1,0:T(8,128)} %stack.31.meta, bf16[4,4,2,128,384]{4,3,2,1,0:T(8,128)(2,1)} %bitcast.17), custom_call_target="tpu_custom_call" | custom-call | tf_op jit(solution)/shard_map/pallas_call | solution.py:325
  63.1 1.3 %copy.15 = f32[32,1,128]{2,1,0:T(1,128)} copy(f32[32,1,128]{2,1,0:T(1,128)} %bitcast.27) | data formatting | bytes 32768
  64.5 1.8 %copy.16 = f32[16,16,384]{2,1,0:T(8,128)} copy(f32[16,16,384]{2,1,0:T(8,128)} %bitcast.18) | data formatting | bytes 786432
  (1 shorter events, 0.0 us)

commit v2 on v1

v2 whole, which is shorter than its diff:
```python
import functools
import math

import jax
import jax.numpy as jnp
from jax import lax
from jax.experimental import pallas as pl
from jax.experimental.pallas import tpu as pltpu
from jax.sharding import PartitionSpec as P

MESH = pl.DeviceIdType.MESH
AWAY = -1000.0


def weight_rows(position, frac, rows):
    ids = lax.broadcasted_iota(jnp.int32, (rows, position.shape[1]), 0).astype(jnp.float32)
    zero = jnp.zeros_like(ids)
    return jnp.where(
        ids == position, 1.0 - frac, jnp.where(ids == position + 1.0, frac, zero)
    )


def kernel(
    lat_n, lon_n, line, rows, cols, tile,
    field, cell_ref, frac_ref, innov_ref, rinv_ref, jac,
    grad_out, dep_out,
    edge, innov, rinv, meta,
    tbl, met, jrecv, dep, grad, gsend, grecv, hrecv,
    t_send, t_recv, m_send, m_recv, j_send, j_recv, d_send, d_recv,
    g_send, g_recv, h_send, h_recv,
):
    inner = lon_n // line
    plane = lat_n * inner
    total = lat_n * lon_n
    slots = jac.shape[3]
    cells = rows * cols
    halo = cells + cols
    lat, lon = lax.axis_index("lat"), lax.axis_index("lon")
    z, xi = lon // inner, lon % inner
    here = lat * inner + xi
    lat_up, lat_down = (lat + 1) % lat_n, (lat + lat_n - 1) % lat_n
    lon_down = (lon + lon_n - 1) % lon_n
    z_low, x_low = lon_down // inner, lon_down % inner

    def remote(src, dst, send, recv, to):
        return pltpu.make_async_remote_copy(
            src_ref=src, dst_ref=dst, send_sem=send, recv_sem=recv,
            device_id=to, device_id_type=MESH,
        )

    def landed(like, sem):
        pltpu.make_async_copy(like, like, sem).wait()

    me = lat * lon_n + lon
    barrier = pltpu.get_barrier_semaphore()

    def greet(i, carry):
        other = (me + i) % total
        pl.semaphore_signal(
            barrier, inc=1, device_id=(other // lon_n, other % lon_n), device_id_type=MESH
        )
        return carry

    lax.fori_loop(1, total, greet, 0)

    mine = pl.ds(here * slots, slots)
    pltpu.make_async_copy(field, tbl.at[z, pl.ds(0, cells)], t_recv.at[z]).start()
    for n in range(line):
        g = (z + 1 + n) % line
        pltpu.make_async_copy(jac.at[lat, g, xi], jrecv.at[g, mine], j_recv.at[g]).start()
    edge[...] = jnp.concatenate(
        [field[pl.ds(r * cols, cols), :].astype(jnp.float32)[0:1] for r in range(rows)], axis=0
    ).astype(edge.dtype)
    innov[...] = innov_ref[...].astype(jnp.float32)
    rinv[...] = rinv_ref[...].astype(jnp.float32)

    def build(k, carry):
        for g in range(line):
            owner = (k // inner) * lon_n + g * inner + k % inner
            cell = cell_ref[owner].astype(jnp.float32)
            live = cell >= 0.0
            row = jnp.floor((cell + 0.5) * (1.0 / (cols + 1)))
            meta[k, g, 0:1] = jnp.where(live, row, AWAY)
            meta[k, g, 1:2] = jnp.where(live, cell - row * (cols + 1), AWAY)
            meta[k, g, 2:4] = frac_ref[owner].astype(jnp.float32)
            meta[k, g, 4:5] = innov[pl.ds(owner, 1), :]
            meta[k, g, 5:6] = rinv[pl.ds(owner, 1), :]
            meta[k, g, 6:8] = jnp.zeros((2, slots), jnp.float32)
        return carry

    lax.fori_loop(0, plane, build, 0)
    pltpu.make_async_copy(meta.at[here], met.at[:, :, mine], m_recv).start()
    pl.semaphore_wait(barrier, total - 1)

    def send_jac(g):
        def one(i, carry):
            to = (here + i) % plane
            remote(
                jac.at[to // inner, g, to % inner], jrecv.at[g, mine], j_send, j_recv.at[g],
                (to // inner, z * inner + to % inner),
            ).start()
            return carry

        lax.fori_loop(1, plane, one, 0)

    def send_meta(i, carry):
        to = (here + i) % plane
        remote(
            meta.at[to], met.at[:, :, mine], m_send, m_recv,
            (to // inner, z * inner + to % inner),
        ).start()
        return carry

    send_jac((z + 1) % line)
    for i in (*range(1, line), 0):
        to = (z + i) % line
        if i > 0:
            remote(field, tbl.at[z, pl.ds(0, cells)], t_send.at[0], t_recv.at[z],
                   (lat, to * inner + xi)).start()
        remote(field.at[pl.ds(0, cols)], tbl.at[z, pl.ds(cells, cols)], t_send.at[1],
               t_recv.at[z], (lat_down, to * inner + xi)).start()
        remote(edge, tbl.at[z_low, pl.ds(halo, rows)], t_send.at[1], t_recv.at[z_low],
               (lat, to * inner + x_low)).start()
        remote(edge, tbl.at[z_low, pl.ds(halo + rows, rows)], t_send.at[1], t_recv.at[z_low],
               (lat_down, to * inner + x_low)).start()
    lax.fori_loop(1, plane, send_meta, 0)
    for n in range(1, line):
        send_jac((z + 1 + n) % line)

    landed(met, m_recv)
    inside = jnp.where(lat < lat_n - 1, 1.0, 0.0)
    width = tile * slots
    tiles = plane // tile
    pad = -(-(max(rows, cols) + 1) // 8) * 8

    def group(n, carry):
        g = (z + 1 + n) % line
        landed(tbl.at[g], t_recv.at[g])
        landed(jrecv.at[g], j_recv.at[g])
        if tiles > 1:
            grad[...] = jnp.zeros_like(grad)

        def one_tile(t, inner_carry):
            lanes = pl.ds(pl.multiple_of(t * width, width), width)
            info = met[g, :, lanes]
            lat_w = weight_rows(info[0:1], info[2:3], pad)
            lon_w = weight_rows(info[1:2], info[3:4], pad)
            lon_c = lon_w[:cols]
            lon_e = lon_w[cols:cols + 1]
            lat_n_row = lat_w[rows:rows + 1] * inside
            first = lax.broadcasted_iota(jnp.int32, (rows, width), 0) == 0
            blocks = [lat_w[r:r + 1] * lon_c for r in range(rows)]
            blocks.append(lat_n_row * lon_c)
            blocks.append(lat_w[:rows] * lon_e)
            blocks.append(
                jnp.where(first, jnp.broadcast_to(lat_n_row * lon_e, (rows, width)), 0.0)
            )
            spread = jnp.concatenate(blocks, axis=0).astype(jnp.bfloat16).astype(jnp.float32)
            jac_t = jrecv[g, lanes]
            products = lax.dot_general(
                tbl[g], jac_t, (((1,), (1,)), ((), ())), preferred_element_type=jnp.float32
            )
            evolved = jnp.sum(spread * products, axis=0, keepdims=True)
            departure = jnp.where(info[0:1] >= 0.0, evolved - info[4:5], 0.0)
            dep[g, :, lanes] = departure
            scaled = (spread * (info[5:6] * departure)).astype(jnp.bfloat16)
            partial = jnp.dot(scaled, jac_t, preferred_element_type=jnp.float32)
            if tiles > 1:
                grad[...] += partial
            else:
                grad[...] = partial
            return inner_carry

        if tiles > 1:
            lax.fori_loop(0, tiles, one_tile, 0)
        else:
            one_tile(0, 0)
        gsend[g] = grad[...].astype(jnp.bfloat16)
        east = (g * inner + xi + 1) % lon_n
        remote(gsend.at[g, pl.ds(cells, cols)], hrecv.at[0, z], h_send, h_recv,
               (lat_up, g * inner + xi)).start()
        remote(gsend.at[g, pl.ds(halo, rows)], hrecv.at[1, z], h_send, h_recv,
               (lat, east)).start()
        remote(gsend.at[g, pl.ds(halo + rows, rows)], hrecv.at[2, z], h_send, h_recv,
               (lat_up, east)).start()

        @pl.when(n < line - 1)
        def _():
            slot = lax.rem(n, line - 1)
            remote(gsend.at[g, pl.ds(0, cells)], grecv.at[slot], g_send, g_recv,
                   (lat, g * inner + xi)).start()

        def send_dep(i, inner_carry):
            to = (here + i) % plane
            remote(
                dep.at[g, :, pl.ds(to * slots, slots)], dep_out.at[lat, g, xi], d_send, d_recv,
                (to // inner, z * inner + to % inner),
            ).start()
            return inner_carry

        lax.fori_loop(1, plane, send_dep, 0)
        pltpu.make_async_copy(dep.at[g, :, mine], dep_out.at[lat, g, xi], d_recv).start()
        return carry

    lax.fori_loop(0, line, group, 0)

    landed(grecv, g_recv)
    field_sum = grad[pl.ds(0, cells), :]
    for slot in range(line - 1):
        field_sum = field_sum + grecv[slot].astype(jnp.float32)
    grad_out[...] = field_sum
    landed(hrecv, h_recv)
    grad_out[pl.ds(0, cols), :] += jnp.sum(hrecv[0].astype(jnp.float32), axis=0)
    east_sum = jnp.sum(hrecv[1].astype(jnp.float32), axis=0)
    corner_sum = jnp.sum(hrecv[2].astype(jnp.float32), axis=0)
    for r in range(rows):
        extra = east_sum[r:r + 1]
        if r == 0:
            extra = extra + corner_sum[0:1]
        grad_out[pl.ds(r * cols, 1), :] += extra

    others = pl.ds(0, (plane - 1) * slots)
    landed(dep_out, d_recv)
    landed(grecv, t_send.at[0])
    landed(tbl.at[:, pl.ds(cells, cols + 2 * rows)], t_send.at[1])
    landed(met.at[:, :, others], m_send)
    landed(jrecv.at[:, others], j_send)
    landed(dep.at[:, :, others], d_send)
    landed(grecv, g_send)
    landed(gsend.at[:, pl.ds(cells, cols + 2 * rows)], h_send)


def shards(mesh_shape, field, obs_jac, obs_frac, obs_innov, obs_rinv, obs_cells):
    lat_n, lon_n = mesh_shape
    line = math.gcd(lon_n // 2, 4)
    inner = lon_n // line
    plane = lat_n * inner
    total = lat_n * lon_n
    rows, cols, wide = field.shape
    slots = obs_jac.shape[2]
    tile = math.gcd(plane, 8)
    cells = rows * cols
    table = cells + cols + 2 * rows
    f32, bf16 = jnp.float32, jnp.bfloat16
    dma = pltpu.SemaphoreType.DMA
    one = pltpu.SemaphoreType.DMA(())
    vmem = pl.BlockSpec(memory_space=pltpu.VMEM)
    grad, departures = pl.pallas_call(
        functools.partial(kernel, lat_n, lon_n, line, rows, cols, tile),
        out_shape=(
            jax.ShapeDtypeStruct((cells, wide), f32),
            jax.ShapeDtypeStruct((lat_n, line, inner, 1, slots), f32),
        ),
        in_specs=[vmem, vmem, vmem, vmem, vmem, pl.BlockSpec(memory_space=pl.ANY)],
        out_specs=(vmem, vmem),
        scratch_shapes=[
            pltpu.VMEM((rows, wide), bf16),
            pltpu.VMEM((total, slots), f32),
            pltpu.VMEM((total, slots), f32),
            pltpu.VMEM((plane, line, 8, slots), f32),
            pltpu.VMEM((line, table, wide), bf16),
            pltpu.VMEM((line, 8, plane * slots), f32),
            pltpu.VMEM((line, plane * slots, wide), bf16),
            pltpu.VMEM((line, 1, plane * slots), f32),
            pltpu.VMEM((table, wide), f32),
            pltpu.VMEM((line, table, wide), bf16),
            pltpu.VMEM((line - 1, cells, wide), bf16),
            pltpu.VMEM((3, line, rows, wide), bf16),
            dma((2,)), dma((line,)),
            one, one,
            one, dma((line,)),
            one, one,
            one, one,
            one, one,
        ],
        compiler_params=pltpu.CompilerParams(
            collective_id=0, has_side_effects=True, vmem_limit_bytes=60 * 1024 * 1024
        ),
    )(
        field.reshape(cells, wide),
        obs_cells,
        obs_frac.reshape(total, 2, slots),
        obs_innov.reshape(total, slots),
        obs_rinv.reshape(total, slots),
        obs_jac.reshape(lat_n, line, inner, slots, wide),
    )
    return (
        departures.reshape(total, 1, slots),
        grad.reshape(rows, cols, wide),
    )


def solution(mesh):
    placed = (
        P("lat", "lon", None),
        P(None, ("lat", "lon"), None, None),
        P(None, ("lat", "lon"), None, None),
        P(None, ("lat", "lon"), None),
        P(None, ("lat", "lon"), None),
        P(None, ("lat", "lon"), None),
    )
    return jax.shard_map(
        functools.partial(shards, (mesh.shape["lat"], mesh.shape["lon"])),
        mesh=mesh,
        in_specs=placed,
        out_specs=(P(None, ("lat", "lon"), None), P("lat", "lon", None)),
        check_vma=False,
    )
```

time: 66.9 us -> 58 us (0.87)
  local copies, waits for them, and re-layouts: 6.25 us -> 3.09 us
  Pallas kernels: 57 us -> 54 us
  other arithmetic: 2.27 us -> 0 us
    pallas_call x1, Pallas kernels: 57 us -> 54 us  [shards(): pl.pallas_call(functools.partial(kernel, lat_n, lon_n, line, rows, cols,...]
    slice x2 -> x0, local copies, waits for them, and re-layouts: 1.73 us -> none  [the longest x1 0.91 us: shards(): field[:, 0]]
    another operation x2 -> x0, other arithmetic: 1.4 us -> none  [shards(): jnp.stack([row_pos, col_pos, obs_frac[:, 0, 0].astype(f32), obs_frac[:, 0...]
    select_n x1 -> x0, other arithmetic: 0.87 us -> none  [shards(): col_pos = jnp.where(live, (ids % (cols + 1)).astype(f32), away)]
    another operation x2 -> x0, local copies, waits for them, and re-layouts: 0.83 us -> none  [shards(): jnp.stack([row_pos, col_pos, obs_frac[:, 0, 0].astype(f32), obs_frac[:, 0...]
    unnamed x3 -> x2, local copies, waits for them, and re-layouts: 3.69 us -> 3.09 us
where the time goes in v2:
time: 58 us; the launch traced here: 57.8 us
  Pallas kernels  54 us (93%)
  local copies, waits for them, and re-layouts  3.09 us (5%)
  between operations  0.64 us (1%)
    pallas_call x1, Pallas kernels, shards(): pl.pallas_call(functools.partial(kernel, lat_n, lon_n, line, rows, cols,...  54 us
    unnamed x2, local copies, waits for them, and re-layouts  3.09 us

profile of v2, /device:TPU:0, one launch (start us, length us, event | category | flops | bytes accessed | tf_op | source)
XLA Modules:
  0.0 57.8 jit_solution(11950452560190923104)
XLA Ops:
  0.6 54.0 %shard_map.77 = (f32[256,384]{1,0:T(8,128)}, f32[4,4,2,1,128]{4,3,2,1,0:T(1,128)}) custom-call(bf16[256,384]{1,0:T(8,128)(2,1)} %bitcast.11, s32[32,1,128]{2,1,0:T(1,128)} %cell_ref.1, bf16[32,2,128]{2,1,0:T(2,128)(2,1)} %bitcast.12, bf16[32,128]{1,0:T(8,128)(2,1)} %bitcast.14, bf16[32,128]{1,0:T(8,128)(2,1)} %bitcast.15, bf16[4,4,2,128,384]{4,3,2,1,0:T(8,128)(2,1)} %bitcast.9), custom_call_target="tpu_custom_call" | custom-call | tf_op jit(solution)/shard_map/pallas_call | solution.py:248
  54.7 1.3 %copy.11 = f32[32,1,128]{2,1,0:T(1,128)} copy(f32[32,1,128]{2,1,0:T(1,128)} %bitcast.13) | data formatting | bytes 32768
  56.0 1.8 %copy.12 = f32[16,16,384]{2,1,0:T(8,128)} copy(f32[16,16,384]{2,1,0:T(8,128)} %bitcast.10) | data formatting | bytes 786432

commit v3 on v2

--- a/solution.py
+++ b/solution.py
@@ -23,11 +23,11 @@
 def kernel(
     lat_n, lon_n, line, rows, cols, tile,
     field, cell_ref, frac_ref, innov_ref, rinv_ref, jac,
-    grad_out, dep_out,
+    grad, grecv, hrecv, dep_out,
     edge, innov, rinv, meta,
-    tbl, met, jrecv, dep, grad, gsend, grecv, hrecv,
+    tbl, met, jrecv, dep, gsend,
     t_send, t_recv, m_send, m_recv, j_send, j_recv, d_send, d_recv,
-    g_send, g_recv, h_send, h_recv,
+    g_send, g_recv, h_send, h_recv, from_low, from_high,
 ):
     inner = lon_n // line
     plane = lat_n * inner
@@ -51,26 +51,87 @@
     def landed(like, sem):
         pltpu.make_async_copy(like, like, sem).wait()
 
-    me = lat * lon_n + lon
+    has_low, has_high = z > 0, z < line - 1
+    low, high = (lat, lon - inner), (lat, lon + inner)
     barrier = pltpu.get_barrier_semaphore()
 
+    @pl.when(has_low)
+    def _():
+        pl.semaphore_signal(barrier, inc=1, device_id=low, device_id_type=MESH)
+
+    @pl.when(has_high)
+    def _():
+        pl.semaphore_signal(barrier, inc=1, device_id=high, device_id_type=MESH)
+
     def greet(i, carry):
-        other = (me + i) % total
+        to = (here + i) % plane
         pl.semaphore_signal(
-            barrier, inc=1, device_id=(other // lon_n, other % lon_n), device_id_type=MESH
+            barrier, inc=1, device_id=(to // inner, z * inner + to % inner), device_id_type=MESH
         )
         return carry
 
-    lax.fori_loop(1, total, greet, 0)
+    lax.fori_loop(1, plane, greet, 0)
 
     mine = pl.ds(here * slots, slots)
     pltpu.make_async_copy(field, tbl.at[z, pl.ds(0, cells)], t_recv.at[z]).start()
     for n in range(line):
         g = (z + 1 + n) % line
         pltpu.make_async_copy(jac.at[lat, g, xi], jrecv.at[g, mine], j_recv.at[g]).start()
+    pl.semaphore_wait(barrier, plane - 1 + has_low.astype(jnp.int32) + has_high.astype(jnp.int32))
+
+    def send_jac(g):
+        def one(i, carry):
+            to = (here + i) % plane
+            remote(
+                jac.at[to // inner, g, to % inner], jrecv.at[g, mine], j_send, j_recv.at[g],
+                (to // inner, z * inner + to % inner),
+            ).start()
+            return carry
+
+        lax.fori_loop(1, plane, one, 0)
+
+    def send_meta(i, carry):
+        to = (here + i) % plane
+        remote(
+            meta.at[to], met.at[:, :, mine], m_send, m_recv,
+            (to // inner, z * inner + to % inner),
+        ).start()
+        return carry
+
+    send_jac((z + 1) % line)
     edge[...] = jnp.concatenate(
         [field[pl.ds(r * cols, cols), :].astype(jnp.float32)[0:1] for r in range(rows)], axis=0
     ).astype(edge.dtype)
+
+    for _ in range(line - 1):
+        @pl.when(has_low)
+        def _():
+            pl.semaphore_signal(from_high, inc=1, device_id=low, device_id_type=MESH)
+
+        @pl.when(has_high)
+        def _():
+            pl.semaphore_signal(from_low, inc=1, device_id=high, device_id_type=MESH)
+
+        @pl.when(has_low)
+        def _():
+            pl.semaphore_wait(from_low, 1)
+
+        @pl.when(has_high)
+        def _():
+            pl.semaphore_wait(from_high, 1)
+
+    for i in (*range(1, line), 0):
+        to = (z + i) % line
+        if i > 0:
+            remote(field, tbl.at[z, pl.ds(0, cells)], t_send.at[0], t_recv.at[z],
+                   (lat, to * inner + xi)).start()
+        remote(field.at[pl.ds(0, cols)], tbl.at[z, pl.ds(cells, cols)], t_send.at[1],
+               t_recv.at[z], (lat_down, to * inner + xi)).start()
+        remote(edge, tbl.at[z_low, pl.ds(halo, rows)], t_send.at[1], t_recv.at[z_low],
+               (lat, to * inner + x_low)).start()
+        remote(edge, tbl.at[z_low, pl.ds(halo + rows, rows)], t_send.at[1], t_recv.at[z_low],
+               (lat_down, to * inner + x_low)).start()
+    send_jac((z + 2) % line)
     innov[...] = innov_ref[...].astype(jnp.float32)
     rinv[...] = rinv_ref[...].astype(jnp.float32)
 
@@ -90,41 +151,9 @@
 
     lax.fori_loop(0, plane, build, 0)
     pltpu.make_async_copy(meta.at[here], met.at[:, :, mine], m_recv).start()
-    pl.semaphore_wait(barrier, total - 1)
-
-    def send_jac(g):
-        def one(i, carry):
-            to = (here + i) % plane
-            remote(
-                jac.at[to // inner, g, to % inner], jrecv.at[g, mine], j_send, j_recv.at[g],
-                (to // inner, z * inner + to % inner),
-            ).start()
-            return carry
-
-        lax.fori_loop(1, plane, one, 0)
-
-    def send_meta(i, carry):
-        to = (here + i) % plane
-        remote(
-            meta.at[to], met.at[:, :, mine], m_send, m_recv,
-            (to // inner, z * inner + to % inner),
-        ).start()
-        return carry
-
-    send_jac((z + 1) % line)
-    for i in (*range(1, line), 0):
-        to = (z + i) % line
-        if i > 0:
-            remote(field, tbl.at[z, pl.ds(0, cells)], t_send.at[0], t_recv.at[z],
-                   (lat, to * inner + xi)).start()
-        remote(field.at[pl.ds(0, cols)], tbl.at[z, pl.ds(cells, cols)], t_send.at[1],
-               t_recv.at[z], (lat_down, to * inner + xi)).start()
-        remote(edge, tbl.at[z_low, pl.ds(halo, rows)], t_send.at[1], t_recv.at[z_low],
-               (lat, to * inner + x_low)).start()
-        remote(edge, tbl.at[z_low, pl.ds(halo + rows, rows)], t_send.at[1], t_recv.at[z_low],
-               (lat_down, to * inner + x_low)).start()
+
     lax.fori_loop(1, plane, send_meta, 0)
-    for n in range(1, line):
+    for n in range(2, line):
         send_jac((z + 1 + n) % line)
 
     landed(met, m_recv)
@@ -204,12 +233,25 @@
 
     lax.fori_loop(0, line, group, 0)
 
+    others = pl.ds(0, (plane - 1) * slots)
     landed(grecv, g_recv)
-    field_sum = grad[pl.ds(0, cells), :]
-    for slot in range(line - 1):
+    landed(hrecv, h_recv)
+    landed(dep_out, d_recv)
+    landed(grecv, t_send.at[0])
+    landed(tbl.at[:, pl.ds(cells, cols + 2 * rows)], t_send.at[1])
+    landed(met.at[:, :, others], m_send)
+    landed(jrecv.at[:, others], j_send)
+    landed(dep.at[:, :, others], d_send)
+    landed(grecv, g_send)
+    landed(gsend.at[:, pl.ds(cells, cols + 2 * rows)], h_send)
+
+
+def last_sums(rows, cols, grad, grecv, hrecv, dep, grad_out, dep_out):
+    dep_out[...] = dep[...]
+    field_sum = grad[pl.ds(0, rows * cols), :]
+    for slot in range(grecv.shape[0]):
         field_sum = field_sum + grecv[slot].astype(jnp.float32)
     grad_out[...] = field_sum
-    landed(hrecv, h_recv)
     grad_out[pl.ds(0, cols), :] += jnp.sum(hrecv[0].astype(jnp.float32), axis=0)
     east_sum = jnp.sum(hrecv[1].astype(jnp.float32), axis=0)
     corner_sum = jnp.sum(hrecv[2].astype(jnp.float32), axis=0)
@@ -218,16 +260,6 @@
         if r == 0:
             extra = extra + corner_sum[0:1]
         grad_out[pl.ds(r * cols, 1), :] += extra
-
-    others = pl.ds(0, (plane - 1) * slots)
-    landed(dep_out, d_recv)
-    landed(grecv, t_send.at[0])
-    landed(tbl.at[:, pl.ds(cells, cols + 2 * rows)], t_send.at[1])
-    landed(met.at[:, :, others], m_send)
-    landed(jrecv.at[:, others], j_send)
-    landed(dep.at[:, :, others], d_send)
-    landed(grecv, g_send)
-    landed(gsend.at[:, pl.ds(cells, cols + 2 * rows)], h_send)
 
 
 def shards(mesh_shape, field, obs_jac, obs_frac, obs_innov, obs_rinv, obs_cells):
@@ -245,14 +277,16 @@
     dma = pltpu.SemaphoreType.DMA
     one = pltpu.SemaphoreType.DMA(())
     vmem = pl.BlockSpec(memory_space=pltpu.VMEM)
-    grad, departures = pl.pallas_call(
+    parts = pl.pallas_call(
         functools.partial(kernel, lat_n, lon_n, line, rows, cols, tile),
         out_shape=(
-            jax.ShapeDtypeStruct((cells, wide), f32),
+            jax.ShapeDtypeStruct((table, wide), f32),
+            jax.ShapeDtypeStruct((line - 1, cells, wide), bf16),
+            jax.ShapeDtypeStruct((3, line, rows, wide), bf16),
             jax.ShapeDtypeStruct((lat_n, line, inner, 1, slots), f32),
         ),
         in_specs=[vmem, vmem, vmem, vmem, vmem, pl.BlockSpec(memory_space=pl.ANY)],
-        out_specs=(vmem, vmem),
+        out_specs=(vmem,) * 4,
         scratch_shapes=[
             pltpu.VMEM((rows, wide), bf16),
             pltpu.VMEM((total, slots), f32),
@@ -262,16 +296,14 @@
             pltpu.VMEM((line, 8, plane * slots), f32),
             pltpu.VMEM((line, plane * slots, wide), bf16),
             pltpu.VMEM((line, 1, plane * slots), f32),
-            pltpu.VMEM((table, wide), f32),
             pltpu.VMEM((line, table, wide), bf16),
-            pltpu.VMEM((line - 1, cells, wide), bf16),
-            pltpu.VMEM((3, line, rows, wide), bf16),
             dma((2,)), dma((line,)),
             one, one,
             one, dma((line,)),
             one, one,
             one, one,
             one, one,
+            pltpu.SemaphoreType.REGULAR, pltpu.SemaphoreType.REGULAR,
         ],
         compiler_params=pltpu.CompilerParams(
             collective_id=0, has_side_effects=True, vmem_limit_bytes=60 * 1024 * 1024
@@ -284,10 +316,16 @@
         obs_rinv.reshape(total, slots),
         obs_jac.reshape(lat_n, line, inner, slots, wide),
     )
-    return (
-        departures.reshape(total, 1, slots),
-        grad.reshape(rows, cols, wide),
-    )
+    grad, departures = pl.pallas_call(
+        functools.partial(last_sums, rows, cols),
+        out_shape=(
+            jax.ShapeDtypeStruct((cells, wide), f32),
+            jax.ShapeDtypeStruct((total, 1, slots), f32),
+        ),
+        in_specs=[vmem] * 4,
+        out_specs=(vmem, vmem),
+    )(*parts[:3], parts[3].reshape(total, 1, slots))
+    return departures, grad.reshape(rows, cols, wide)
 
 
 def solution(mesh):

time: 58 us -> 56.4 us (0.972)
  local copies, waits for them, and re-layouts: 3.09 us -> 0 us
  Pallas kernels: 54 us -> 55.6 us
    unnamed x2 -> x0, local copies, waits for them, and re-layouts: 3.09 us -> none
    pallas_call x0 -> x1, Pallas kernels: none -> 2.12 us  [shards(): pl.pallas_call(functools.partial(last_sums, rows, cols), out_shape=(jax.S...]
where the time goes in v3:
time: 56.4 us; the launch traced here: 56.2 us
  Pallas kernels  55.6 us (99%)
  between operations  0.64 us (1%)
    pallas_call x1, Pallas kernels, shards(): pl.pallas_call(functools.partial(kernel, lat_n, lon_n, line, rows, cols,...  53.5 us
    pallas_call x1, Pallas kernels, shards(): pl.pallas_call(functools.partial(last_sums, rows, cols), out_shape=(jax.S...  2.12 us

profile of v3, /device:TPU:0, one launch (start us, length us, event | category | flops | bytes accessed | tf_op | source)
XLA Modules:
  0.0 56.2 jit_solution(5933351421806763855)
XLA Ops:
  0.6 53.5 %shard_map.77 = (f32[304,384]{1,0:T(8,128)}, bf16[3,256,384]{2,1,0:T(8,128)(2,1)}, bf16[3,4,16,384]{3,2,1,0:T(8,128)(2,1)}, f32[4,4,2,1,128]{4,3,2,1,0:T(1,128)}) custom-call(bf16[256,384]{1,0:T(8,128)(2,1)} %bitcast.8, s32[32,1,128]{2,1,0:T(1,128)} %cell_ref.1, bf16[32,2,128]{2,1,0:T(2,128)(2,1)} %bitcast.9, bf16[32,128]{1,0:T(8,128)(2,1)} %bitcast.11, ...), custom_call_target="tpu_custom_call" | custom-call | tf_op jit(solution)/shard_map/pallas_call | solution.py:280
  54.1 2.1 %shard_map.78 = (f32[256,384]{1,0:T(8,128)}, f32[32,1,128]{2,1,0:T(1,128)}) custom-call(f32[304,384]{1,0:T(8,128)} %get-tuple-element.8.grad, bf16[3,256,384]{2,1,0:T(8,128)(2,1)} %get-tuple-element.9.grecv, bf16[3,4,16,384]{3,2,1,0:T(8,128)(2,1)} %get-tuple-element.10.hrecv, f32[32,1,128]{2,1,0:T(1,128)} %bitcast.10), custom_call_target="tpu_custom_call" | custom-call | tf_op jit(solution)/shard_map/pallas_call | solution.py:319

commit v4 on v3

--- a/solution.py
+++ b/solution.py
@@ -26,7 +26,7 @@
     grad, grecv, hrecv, dep_out,
     edge, innov, rinv, meta,
     tbl, met, jrecv, dep, gsend,
-    t_send, t_recv, m_send, m_recv, j_send, j_recv, d_send, d_recv,
+    e_send, t_send, t_recv, m_send, m_recv, j_send, j_recv, d_send, d_recv,
     g_send, g_recv, h_send, h_recv, from_low, from_high,
 ):
     inner = lon_n // line
@@ -42,6 +42,11 @@
     lon_down = (lon + lon_n - 1) % lon_n
     z_low, x_low = lon_down // inner, lon_down % inner
 
+    step = 2 * (2 * z < line).astype(jnp.int32) - 1
+
+    def band(n):
+        return (z + step * (n + 1) + line) % line
+
     def remote(src, dst, send, recv, to):
         return pltpu.make_async_remote_copy(
             src_ref=src, dst_ref=dst, send_sem=send, recv_sem=recv,
@@ -75,7 +80,7 @@
     mine = pl.ds(here * slots, slots)
     pltpu.make_async_copy(field, tbl.at[z, pl.ds(0, cells)], t_recv.at[z]).start()
     for n in range(line):
-        g = (z + 1 + n) % line
+        g = band(n)
         pltpu.make_async_copy(jac.at[lat, g, xi], jrecv.at[g, mine], j_recv.at[g]).start()
     pl.semaphore_wait(barrier, plane - 1 + has_low.astype(jnp.int32) + has_high.astype(jnp.int32))
 
@@ -98,12 +103,12 @@
         ).start()
         return carry
 
-    send_jac((z + 1) % line)
+    send_jac(band(0))
     edge[...] = jnp.concatenate(
         [field[pl.ds(r * cols, cols), :].astype(jnp.float32)[0:1] for r in range(rows)], axis=0
     ).astype(edge.dtype)
 
-    for _ in range(line - 1):
+    for turn in range(line - 1):
         @pl.when(has_low)
         def _():
             pl.semaphore_signal(from_high, inc=1, device_id=low, device_id_type=MESH)
@@ -120,18 +125,41 @@
         def _():
             pl.semaphore_wait(from_high, 1)
 
-    for i in (*range(1, line), 0):
-        to = (z + i) % line
-        if i > 0:
-            remote(field, tbl.at[z, pl.ds(0, cells)], t_send.at[0], t_recv.at[z],
-                   (lat, to * inner + xi)).start()
-        remote(field.at[pl.ds(0, cols)], tbl.at[z, pl.ds(cells, cols)], t_send.at[1],
-               t_recv.at[z], (lat_down, to * inner + xi)).start()
-        remote(edge, tbl.at[z_low, pl.ds(halo, rows)], t_send.at[1], t_recv.at[z_low],
-               (lat, to * inner + x_low)).start()
-        remote(edge, tbl.at[z_low, pl.ds(halo + rows, rows)], t_send.at[1], t_recv.at[z_low],
-               (lat_down, to * inner + x_low)).start()
-    send_jac((z + 2) % line)
+        if turn == 0:
+            remote(field.at[pl.ds(0, cols)], tbl.at[z, pl.ds(cells, cols)], e_send,
+                   t_recv.at[z], (lat_down, lon)).start()
+        if turn == line - 2:
+            remote(edge, tbl.at[z_low, pl.ds(halo, rows)], e_send, t_recv.at[z_low],
+                   (lat, lon_down)).start()
+            remote(edge, tbl.at[z_low, pl.ds(halo + rows, rows)], e_send, t_recv.at[z_low],
+                   (lat_down, lon_down)).start()
+
+    def to_high(slot):
+        return remote(tbl.at[slot], tbl.at[slot], t_send.at[0, slot], t_recv.at[slot], high)
+
+    def to_low(slot):
+        return remote(tbl.at[slot], tbl.at[slot], t_send.at[1, slot], t_recv.at[slot], low)
+
+    def pass_on(n):
+        below, above = z - n - 1, z + n + 1
+
+        @pl.when(below >= 0)
+        def _():
+            landed(tbl.at[below], t_recv.at[below])
+
+            @pl.when(has_high)
+            def _():
+                to_high(below).start()
+
+        @pl.when(above < line)
+        def _():
+            landed(tbl.at[above], t_recv.at[above])
+
+            @pl.when(has_low)
+            def _():
+                to_low(above).start()
+
+    send_jac(band(1))
     innov[...] = innov_ref[...].astype(jnp.float32)
     rinv[...] = rinv_ref[...].astype(jnp.float32)
 
@@ -141,20 +169,35 @@
             cell = cell_ref[owner].astype(jnp.float32)
             live = cell >= 0.0
             row = jnp.floor((cell + 0.5) * (1.0 / (cols + 1)))
-            meta[k, g, 0:1] = jnp.where(live, row, AWAY)
-            meta[k, g, 1:2] = jnp.where(live, cell - row * (cols + 1), AWAY)
-            meta[k, g, 2:4] = frac_ref[owner].astype(jnp.float32)
-            meta[k, g, 4:5] = innov[pl.ds(owner, 1), :]
-            meta[k, g, 5:6] = rinv[pl.ds(owner, 1), :]
-            meta[k, g, 6:8] = jnp.zeros((2, slots), jnp.float32)
+            meta[k, g] = jnp.concatenate(
+                [
+                    jnp.where(live, row, AWAY),
+                    jnp.where(live, cell - row * (cols + 1), AWAY),
+                    frac_ref[owner].astype(jnp.float32),
+                    innov[pl.ds(owner, 1), :],
+                    rinv[pl.ds(owner, 1), :],
+                    jnp.zeros((2, slots), jnp.float32),
+                ],
+                axis=0,
+            ).astype(meta.dtype)
         return carry
 
     lax.fori_loop(0, plane, build, 0)
     pltpu.make_async_copy(meta.at[here], met.at[:, :, mine], m_recv).start()
 
+    landed(tbl.at[z], t_recv.at[z])
+
+    @pl.when(has_high)
+    def _():
+        to_high(z).start()
+
+    @pl.when(has_low)
+    def _():
+        to_low(z).start()
+
     lax.fori_loop(1, plane, send_meta, 0)
     for n in range(2, line):
-        send_jac((z + 1 + n) % line)
+        send_jac(band(n))
 
     landed(met, m_recv)
     inside = jnp.where(lat < lat_n - 1, 1.0, 0.0)
@@ -163,15 +206,19 @@
     pad = -(-(max(rows, cols) + 1) // 8) * 8
 
     def group(n, carry):
-        g = (z + 1 + n) % line
-        landed(tbl.at[g], t_recv.at[g])
+        g = band(n)
+
+        @pl.when(n < line - 1)
+        def _():
+            pass_on(n)
+
         landed(jrecv.at[g], j_recv.at[g])
         if tiles > 1:
             grad[...] = jnp.zeros_like(grad)
 
         def one_tile(t, inner_carry):
             lanes = pl.ds(pl.multiple_of(t * width, width), width)
-            info = met[g, :, lanes]
+            info = met[g, :, lanes].astype(jnp.float32)
             lat_w = weight_rows(info[0:1], info[2:3], pad)
             lon_w = weight_rows(info[1:2], info[3:4], pad)
             lon_c = lon_w[:cols]
@@ -215,7 +262,7 @@
 
         @pl.when(n < line - 1)
         def _():
-            slot = lax.rem(n, line - 1)
+            slot = (g - z - 1 + line) % line
             remote(gsend.at[g, pl.ds(0, cells)], grecv.at[slot], g_send, g_recv,
                    (lat, g * inner + xi)).start()
 
@@ -237,8 +284,16 @@
     landed(grecv, g_recv)
     landed(hrecv, h_recv)
     landed(dep_out, d_recv)
-    landed(grecv, t_send.at[0])
-    landed(tbl.at[:, pl.ds(cells, cols + 2 * rows)], t_send.at[1])
+    landed(tbl.at[0, pl.ds(cells, cols + 2 * rows)], e_send)
+    for slot in range(line):
+        @pl.when(jnp.logical_and(has_high, z >= slot))
+        def _():
+            landed(tbl.at[slot], t_send.at[0, slot])
+
+        @pl.when(jnp.logical_and(has_low, z <= slot))
+        def _():
+            landed(tbl.at[slot], t_send.at[1, slot])
+
     landed(met.at[:, :, others], m_send)
     landed(jrecv.at[:, others], j_send)
     landed(dep.at[:, :, others], d_send)
@@ -291,13 +346,13 @@
             pltpu.VMEM((rows, wide), bf16),
             pltpu.VMEM((total, slots), f32),
             pltpu.VMEM((total, slots), f32),
-            pltpu.VMEM((plane, line, 8, slots), f32),
+            pltpu.VMEM((plane, line, 8, slots), bf16),
             pltpu.VMEM((line, table, wide), bf16),
-            pltpu.VMEM((line, 8, plane * slots), f32),
+            pltpu.VMEM((line, 8, plane * slots), bf16),
             pltpu.VMEM((line, plane * slots, wide), bf16),
             pltpu.VMEM((line, 1, plane * slots), f32),
             pltpu.VMEM((line, table, wide), bf16),
-            dma((2,)), dma((line,)),
+            one, dma((2, line)), dma((line,)),
             one, one,
             one, dma((line,)),
             one, one,

time: 56.4 us -> 60.1 us (1.066)
  Pallas kernels: 55.6 us -> 59.3 us
    pallas_call x1, Pallas kernels: 53.5 us -> 57.1 us  [shards(): pl.pallas_call(functools.partial(kernel, lat_n, lon_n, line, rows, cols,...]
where the time goes in v4:
time: 60.1 us; the launch traced here: 59.9 us
  Pallas kernels  59.3 us (99%)
  between operations  0.64 us (1%)
    pallas_call x1, Pallas kernels, shards(): pl.pallas_call(functools.partial(kernel, lat_n, lon_n, line, rows, cols,...  57.1 us
    pallas_call x1, Pallas kernels, shards(): pl.pallas_call(functools.partial(last_sums, rows, cols), out_shape=(jax.S...  2.12 us

profile of v4, /device:TPU:0, one launch (start us, length us, event | category | flops | bytes accessed | tf_op | source)
XLA Modules:
  0.0 59.9 jit_solution(11127408681263601109)
XLA Ops:
  0.6 57.1 %shard_map.77 = (f32[304,384]{1,0:T(8,128)}, bf16[3,256,384]{2,1,0:T(8,128)(2,1)}, bf16[3,4,16,384]{3,2,1,0:T(8,128)(2,1)}, f32[4,4,2,1,128]{4,3,2,1,0:T(1,128)}) custom-call(bf16[256,384]{1,0:T(8,128)(2,1)} %bitcast.8, s32[32,1,128]{2,1,0:T(1,128)} %cell_ref.1, bf16[32,2,128]{2,1,0:T(2,128)(2,1)} %bitcast.9, bf16[32,128]{1,0:T(8,128)(2,1)} %bitcast.11, ...), custom_call_target="tpu_custom_call" | custom-call | tf_op jit(solution)/shard_map/pallas_call | solution.py:335
  57.8 2.1 %shard_map.78 = (f32[256,384]{1,0:T(8,128)}, f32[32,1,128]{2,1,0:T(1,128)}) custom-call(f32[304,384]{1,0:T(8,128)} %get-tuple-element.8.grad, bf16[3,256,384]{2,1,0:T(8,128)(2,1)} %get-tuple-element.9.grecv, bf16[3,4,16,384]{3,2,1,0:T(8,128)(2,1)} %get-tuple-element.10.hrecv, f32[32,1,128]{2,1,0:T(1,128)} %bitcast.10), custom_call_target="tpu_custom_call" | custom-call | tf_op jit(solution)/shard_map/pallas_call | solution.py:374

commit v5 on v3

--- a/solution.py
+++ b/solution.py
@@ -141,12 +141,17 @@
             cell = cell_ref[owner].astype(jnp.float32)
             live = cell >= 0.0
             row = jnp.floor((cell + 0.5) * (1.0 / (cols + 1)))
-            meta[k, g, 0:1] = jnp.where(live, row, AWAY)
-            meta[k, g, 1:2] = jnp.where(live, cell - row * (cols + 1), AWAY)
-            meta[k, g, 2:4] = frac_ref[owner].astype(jnp.float32)
-            meta[k, g, 4:5] = innov[pl.ds(owner, 1), :]
-            meta[k, g, 5:6] = rinv[pl.ds(owner, 1), :]
-            meta[k, g, 6:8] = jnp.zeros((2, slots), jnp.float32)
+            meta[k, g] = jnp.concatenate(
+                [
+                    jnp.where(live, row, AWAY),
+                    jnp.where(live, cell - row * (cols + 1), AWAY),
+                    frac_ref[owner].astype(jnp.float32),
+                    innov[pl.ds(owner, 1), :],
+                    rinv[pl.ds(owner, 1), :],
+                    jnp.zeros((2, slots), jnp.float32),
+                ],
+                axis=0,
+            ).astype(meta.dtype)
         return carry
 
     lax.fori_loop(0, plane, build, 0)
@@ -171,7 +176,7 @@
 
         def one_tile(t, inner_carry):
             lanes = pl.ds(pl.multiple_of(t * width, width), width)
-            info = met[g, :, lanes]
+            info = met[g, :, lanes].astype(jnp.float32)
             lat_w = weight_rows(info[0:1], info[2:3], pad)
             lon_w = weight_rows(info[1:2], info[3:4], pad)
             lon_c = lon_w[:cols]
@@ -291,9 +296,9 @@
             pltpu.VMEM((rows, wide), bf16),
             pltpu.VMEM((total, slots), f32),
             pltpu.VMEM((total, slots), f32),
-            pltpu.VMEM((plane, line, 8, slots), f32),
+            pltpu.VMEM((plane, line, 8, slots), bf16),
             pltpu.VMEM((line, table, wide), bf16),
-            pltpu.VMEM((line, 8, plane * slots), f32),
+            pltpu.VMEM((line, 8, plane * slots), bf16),
             pltpu.VMEM((line, plane * slots, wide), bf16),
             pltpu.VMEM((line, 1, plane * slots), f32),
             pltpu.VMEM((line, table, wide), bf16),

time: 56.4 us -> 55.7 us (0.988)
  Pallas kernels: 55.6 us -> 54.9 us
    pallas_call x1, Pallas kernels: 53.5 us -> 52.8 us  [shards(): pl.pallas_call(functools.partial(kernel, lat_n, lon_n, line, rows, cols,...]
where the time goes in v5:
time: 55.7 us; the launch traced here: 55.6 us
  Pallas kernels  54.9 us (99%)
  between operations  0.64 us (1%)
    pallas_call x1, Pallas kernels, shards(): pl.pallas_call(functools.partial(kernel, lat_n, lon_n, line, rows, cols,...  52.8 us
    pallas_call x1, Pallas kernels, shards(): pl.pallas_call(functools.partial(last_sums, rows, cols), out_shape=(jax.S...  2.12 us

profile of v5, /device:TPU:0, one launch (start us, length us, event | category | flops | bytes accessed | tf_op | source)
XLA Modules:
  0.0 55.6 jit_solution(4337480725784569001)
XLA Ops:
  0.6 52.8 %shard_map.77 = (f32[304,384]{1,0:T(8,128)}, bf16[3,256,384]{2,1,0:T(8,128)(2,1)}, bf16[3,4,16,384]{3,2,1,0:T(8,128)(2,1)}, f32[4,4,2,1,128]{4,3,2,1,0:T(1,128)}) custom-call(bf16[256,384]{1,0:T(8,128)(2,1)} %bitcast.8, s32[32,1,128]{2,1,0:T(1,128)} %cell_ref.1, bf16[32,2,128]{2,1,0:T(2,128)(2,1)} %bitcast.9, bf16[32,128]{1,0:T(8,128)(2,1)} %bitcast.11, ...), custom_call_target="tpu_custom_call" | custom-call | tf_op jit(solution)/shard_map/pallas_call | solution.py:285
  53.4 2.1 %shard_map.78 = (f32[256,384]{1,0:T(8,128)}, f32[32,1,128]{2,1,0:T(1,128)}) custom-call(f32[304,384]{1,0:T(8,128)} %get-tuple-element.8.grad, bf16[3,256,384]{2,1,0:T(8,128)(2,1)} %get-tuple-element.9.grecv, bf16[3,4,16,384]{3,2,1,0:T(8,128)(2,1)} %get-tuple-element.10.hrecv, f32[32,1,128]{2,1,0:T(1,128)} %bitcast.10), custom_call_target="tpu_custom_call" | custom-call | tf_op jit(solution)/shard_map/pallas_call | solution.py:324
